TPU v7x, 256 devices: a whole 4x4x8 slice. The times are simulated.
256 devices in a mesh: seq: 128 (over z, x, y_lo, core), sec: 2 (over y_hi).
Axes of the slice: x: 4, y: 4 (y_hi: 2, y_lo: 2; y = y_hi * 2 + y_lo), z: 8, core: 2. Of those that a mesh axis runs over, the one named last changes fastest.
Arguments:
- queries: bfloat16 [2, 2048, 64, 3072], P('sec', 'seq'), may hold values from -250 to 250
- encoded: bfloat16 [2, 1024, 32, 512], P('sec', 'seq'), may hold values from -6 to 6
- neighbours: int32 [2, 2048, 2], P('sec', 'seq'), may hold values from 0 to 1023, as said below
- kv_weight: bfloat16 [2, 512, 3072], P(None, None, 'seq'), may hold values from -0.25 to 0.25
Outputs:
- attended: bfloat16 [2, 2048, 64, 3072], P('sec', 'seq')
Inputs may be any that keep to these rules, and one draw needn't show every extreme that they name: Block id b lies on index b // 8 of seq. The spans held by one device of seq name at most 1 neighbours on any one index of seq, and in every draw some indices of seq receive exactly 1 from every device.
All inputs are finite; a program needn't handle non-finite values.
Results may differ from a plain program's by a relative error of at most 0.012.
Values may be sent and summed in bfloat16 or wider, within the bound.
No kernel may reach another device: no remote copies, remote signals or barrier semaphores. Data moves between devices by JAX's collectives and lax.ppermute only.
A program may use at most 128 MiB of HBM per device.

v0:
```python
import jax
import jax.numpy as jnp
from jax import lax
from jax.sharding import PartitionSpec as P

HDIM = 128


def from_partner(shard, axis, distance):
    return lax.ppermute(shard, axis, [(i, i ^ 1 << distance) for i in range(lax.axis_size(axis))])


def fetch_rows(block_ids, store, owners, slots_each, blocks_each):
    owner = block_ids // blocks_each
    local = block_ids % blocks_each
    owner_match = (owner[:, None] == jnp.arange(owners)[None, :]).astype(jnp.int32)
    rank = jnp.sum(jnp.cumsum(owner_match, 0) * owner_match, 1) - 1
    slot = owner * slots_each + rank
    placed = (slot[:, None] == jnp.arange(owners * slots_each)[None, :]).astype(jnp.int32)
    request = jnp.sum(placed * local[:, None], 0).reshape(owners, slots_each)
    asked = lax.all_to_all(request, "seq", split_axis=0, concat_axis=0, tiled=True)
    rows = store[asked.reshape(-1)].reshape(asked.shape + store.shape[1:])
    replies = lax.all_to_all(rows, "seq", split_axis=0, concat_axis=0, tiled=True)
    flat = replies.reshape((owners * slots_each,) + store.shape[1:])
    return flat[slot]


def body(queries, encoded, neighbours, kv_weight):
    owners = lax.axis_size("seq")
    span_count = queries.shape[1]
    blocks_each = encoded.shape[1]
    token_count = encoded.shape[2]
    width = encoded.shape[3]
    slots_each = (2 * span_count + owners - 1) // owners
    store = encoded[0]
    block_ids = neighbours[0].reshape(-1)
    remote = from_partner(store, "sec", 0)
    fetched = fetch_rows(block_ids, remote, owners, slots_each, blocks_each)
    rows = fetched.reshape(-1, width)
    piece = lax.all_gather(kv_weight, "seq", axis=2, tiled=True)
    keys = jnp.dot(rows, piece[0], preferred_element_type=jnp.float32).astype(jnp.bfloat16)
    values = jnp.dot(rows, piece[1], preferred_element_type=jnp.float32).astype(jnp.bfloat16)
    projected = jnp.stack([keys, values])
    features = queries.shape[3]
    heads = features // HDIM
    keys = projected[0].reshape(span_count, 2 * token_count, heads, HDIM)
    values = projected[1].reshape(span_count, 2 * token_count, heads, HDIM)
    query_block = queries[0].reshape(span_count, queries.shape[2], heads, HDIM)
    scores = jnp.einsum(
        "cthd,cuhd->chtu", query_block, keys, preferred_element_type=jnp.float32
    ) * HDIM ** (-0.5)
    probs = jax.nn.softmax(scores, axis=-1).astype(jnp.bfloat16)
    mixed = jnp.einsum("chtu,cuhd->cthd", probs, values, preferred_element_type=jnp.float32)
    return mixed.astype(jnp.bfloat16).reshape(1, span_count, queries.shape[2], features)


def solution(mesh):
    placed = (
        P("sec", "seq", None, None),
        P("sec", "seq", None, None),
        P("sec", "seq", None),
        P(None, None, "seq"),
    )
    return jax.shard_map(
        body, mesh=mesh, in_specs=placed, out_specs=P("sec", "seq", None, None), check_vma=False
    )
```

profile of v0, /device:TPU:98, one launch (start us, length us, event | category | flops | bytes accessed | tf_op | source)
XLA Modules:
  0.0 338.0 jit_solution(252661657235599470)
XLA Ops:
  6.5 0.0 all-gather.2.cloned.1.call-start
  6.5 0.7 all-gather.2.cloned.1.call-update
  7.3 0.8 copy.26
  8.0 0.1 reshape_squeeze.8
  8.1 0.1 fusion.15
  8.2 0.1 reduce_window_sum.11
  8.2 0.2 select_reduce_fusion.1
  8.4 0.1 select_reduce_fusion
  8.5 0.8 copy.27
  9.3 12.7 %all-to-all-start = ((s32[128,1,1]{2,1,0:T(1,128)}), s32[128,1,1]{2,1,0:T(1,128)S(1)}, u32[]{:S(2)}, u32[]{:S(2)}) async-start(s32[128,1,1]{2,1,0:T(1,128)} %copy.27), calls=%async_computation | async-start | bytes 131072 | tf_op jit(solution)/shard_map/all_to_all | solution.py:21
  22.0 3.0 collective-permute-start
  25.0 4.2 %all-to-all-done = s32[128,1,1]{2,1,0:T(1,128)S(1)} async-done(((s32[128,1,1]{2,1,0:T(1,128)}), s32[128,1,1]{2,1,0:T(1,128)S(1)}, u32[]{:S(2)}, u32[]{:S(2)}) %all-to-all-start) | async-done | bytes 544 | tf_op jit(solution)/shard_map/all_to_all | solution.py:21
  29.1 2.3 reduce
  31.5 1.1 collective-permute-done
  32.6 2.9 gather_fusion
  35.5 13.3 %all-to-all-start.1 = ((bf16[128,1,32,512]{3,2,1,0:T(8,128)(2,1)}), bf16[128,1,32,512]{3,2,1,0:T(8,128)(2,1)}, u32[]{:S(2)}, u32[]{:S(2)}) async-start(bf16[128,1,32,512]{3,2,1,0:T(8,128)(2,1)} %bitcast.55), calls=%async_computation.1 | async-start | bytes 8388608 | tf_op jit(solution)/shard_map/all_to_all | solution.py:23
  48.8 0.1 reshape_squeeze.9
  48.9 7.4 %copy.37 = bf16[128,8,24,128]{3,2,1,0:T(8,128)(2,1)} copy(bf16[128,8,24,128]{3,1,2,0:T(8,128)(2,1)} %bitcast.56) | data formatting | bytes 12582912
  56.4 99.4 %all-to-all-done.1 = bf16[128,1,32,512]{3,2,1,0:T(8,128)(2,1)} async-done(((bf16[128,1,32,512]{3,2,1,0:T(8,128)(2,1)}), bf16[128,1,32,512]{3,2,1,0:T(8,128)(2,1)}, u32[]{:S(2)}, u32[]{:S(2)}) %all-to-all-start.1) | async-done | bytes 4194336 | tf_op jit(solution)/shard_map/all_to_all | solution.py:23
  155.8 2.8 gather_fusion.1
  158.6 0.0 copy-start
  158.6 98.4 %all-gather.2.cloned.1.call-done = bf16[2,512,3072]{1,2,0:T(8,128)(2,1)} async-done(((bf16[2,512,24]{1,2,0:T(8,128)(2,1)}), bf16[2,512,3072]{1,2,0:T(8,128)(2,1)}) %all-gather.2.cloned.1.call-update) | async-done | bytes 6291472 | tf_op jit(solution)/shard_map/all_gather | solution.py:40
  257.0 0.0 copy-done
  257.0 5.6 %convert_bitcast_fusion.2 = bf16[128,8,24,128]{3,1,2,0:T(8,128)(2,1)S(1)} fusion(bf16[1024,512]{1,0:T(8,128)(2,1)S(1)} %bitcast.58, bf16[2,512,3072]{1,2,0:T(8,128)(2,1)} %all-gather.2.cloned.1.call-done), kind=kOutput, calls=%fused_computation.18 | convolution fusion | flops 3224371200 | bytes 10485760 | tf_op jit(solution)/shard_map/dot_general | solution.py:42
  262.6 0.0 copy-start.1
  262.6 0.0 slice-start
  262.6 4.7 %copy.35 = bf16[128,8,24,128]{3,2,1,0:T(8,128)(2,1)} copy(bf16[128,8,24,128]{3,1,2,0:T(8,128)(2,1)S(1)} %convert_bitcast_fusion.2) | data formatting | bytes 12582912
  267.3 0.0 copy-done.1
  267.3 0.0 slice-start.1
  267.3 5.9 %convert_bitcast_fusion.1 = bf16[128,8,24,128]{3,1,2,0:T(8,128)(2,1)S(1)} fusion(bf16[1024,512]{1,0:T(8,128)(2,1)S(1)} %bitcast.59, bf16[2,512,3072]{1,2,0:T(8,128)(2,1)} %all-gather.2.cloned.1.call-done), kind=kOutput, calls=%fused_computation.17 | convolution fusion | flops 3224371200 | bytes 10485760 | tf_op jit(solution)/shard_map/dot_general | solution.py:41
  273.2 4.6 %copy.36 = bf16[128,8,24,128]{3,2,1,0:T(8,128)(2,1)} copy(bf16[128,8,24,128]{3,1,2,0:T(8,128)(2,1)S(1)} %convert_bitcast_fusion.1) | data formatting | bytes 12582912
  277.8 0.0 slice-done
  277.8 0.0 slice-done.1
  277.8 10.8 %fusion.8 = f32[16,24,64,64]{3,2,1,0:T(8,128)} fusion(bf16[16,64,24,128]{3,2,1,0:T(8,128)(2,1)S(1)} %bitcast.53, bf16[16,64,24,128]{3,2,1,0:T(8,128)(2,1)} %bitcast.54), kind=kOutput, calls=%fused_computation.11 | convolution fusion | flops 402653184 | bytes 18874368 | tf_op jit(solution)/shard_map/cthd,cuhd->chtu/dot_general | solution.py:49
  288.5 16.3 %fusion.19 = (f32[16,24,64]{2,1,0:T(8,128)S(1)}, f32[16,24,64,64]{2,3,1,0:T(8,128)}) fusion(f32[16,24,64,64]{3,2,1,0:T(8,128)} %fusion.8), kind=kOutput, calls=%fused_computation.44 | output fusion | flops 6291519 | bytes 12681216 | tf_op jit(solution)/shard_map/sub | solution.py:52
  304.8 8.1 %convert_bitcast_fusion = bf16[16,64,24,128]{3,1,2,0:T(8,128)(2,1)S(1)} fusion(f32[16,24,64,64]{2,3,1,0:T(8,128)} %get-tuple-element.8, f32[16,24,64]{2,1,0:T(8,128)S(1)} %get-tuple-element.7, bf16[16,64,24,128]{3,2,1,0:T(8,128)(2,1)} %bitcast.57), kind=kOutput, calls=%fused_computation.14 | convolution fusion | flops 408944640 | bytes 18972672 | tf_op jit(solution)/shard_map/chtu,cuhd->cthd/dot_general | solution.py:53
  312.9 8.0 %copy.33 = bf16[16,64,24,128]{3,2,1,0:T(8,128)(2,1)} copy(bf16[16,64,24,128]{3,1,2,0:T(8,128)(2,1)S(1)} %convert_bitcast_fusion) | data formatting | bytes 12582912 | tf_op jit(solution)/shard_map/convert_element_type | solution.py:54
  320.9 10.3 %reshape.181 = bf16[1,16,64,3072]{3,2,1,0:T(8,128)(2,1)} reshape(bf16[16,64,24,128]{3,2,1,0:T(8,128)(2,1)} %copy.33) | data formatting | bytes 12582912 | tf_op jit(solution)/shard_map/reshape | solution.py:54
  (7 shorter events, 0.1 us)
Async XLA Ops:
  6.5 250.5 %all-gather.2.cloned.1.call-start = ((), (), s32[]{:S(2)}) async-start(), calls=%async_computation.2 | async-start | bytes 6340608 | tf_op jit(solution)/shard_map/all_gather | solution.py:40
  9.3 19.9 %all-to-all-start = ((s32[128,1,1]{2,1,0:T(1,128)}), s32[128,1,1]{2,1,0:T(1,128)S(1)}, u32[]{:S(2)}, u32[]{:S(2)}) async-start(s32[128,1,1]{2,1,0:T(1,128)} %copy.27), calls=%async_computation | async-start | bytes 131072 | tf_op jit(solution)/shard_map/all_to_all | solution.py:21
  22.0 10.7 %collective-permute-start = (bf16[8,32,512]{2,1,0:T(8,128)(2,1)}, bf16[8,32,512]{2,1,0:T(8,128)(2,1)S(1)}, u32[]{:S(2)}, u32[]{:S(2)}) collective-permute-start(bf16[8,32,512]{2,1,0:T(8,128)(2,1)} %bitcast.61), channel_id=1, source_target_pairs={{0,1},{1,0},{2,3},{3,2},{4,5},{5,4},{6,7},{7,6},{8,9},{9,8},{10,11... | collective-permute-start | bytes 786440 | tf_op jit(solution)/shard_map/ppermute | solution.py:10
  35.5 120.3 %all-to-all-start.1 = ((bf16[128,1,32,512]{3,2,1,0:T(8,128)(2,1)}), bf16[128,1,32,512]{3,2,1,0:T(8,128)(2,1)}, u32[]{:S(2)}, u32[]{:S(2)}) async-start(bf16[128,1,32,512]{3,2,1,0:T(8,128)(2,1)} %bitcast.55), calls=%async_computation.1 | async-start | bytes 8388608 | tf_op jit(solution)/shard_map/all_to_all | solution.py:23
  158.6 98.4 %copy-start = (bf16[32,32,512]{2,1,0:T(8,128)(2,1)}, bf16[32,32,512]{2,1,0:T(8,128)(2,1)S(1)}, u32[]{:S(2)}) copy-start(bf16[32,32,512]{2,1,0:T(8,128)(2,1)S(1)} %gather_fusion.1) | copy-start | bytes 3145732
  262.6 4.7 %copy-start.1 = (bf16[32,32,512]{2,1,0:T(8,128)(2,1)S(1)}, bf16[32,32,512]{2,1,0:T(8,128)(2,1)}, u32[]{:S(2)}) copy-start(bf16[32,32,512]{2,1,0:T(8,128)(2,1)} %copy-done) | copy-start | bytes 3145732
  262.6 15.2 %slice-start = ((s8[6291456]{0:T(1024)(128)(4,1)}), s8[4194304]{0:T(1024)(128)(4,1)S(1)}, s32[]{:S(2)}) async-start(s8[6291456]{0:T(1024)(128)(4,1)} %bitcast.51), calls=%async_computation.3 | async-start | bytes 8388608
  267.3 10.5 %slice-start.1 = ((s8[6291456]{0:T(1024)(128)(4,1)}), s8[2097152]{0:T(1024)(128)(4,1)S(1)}, s32[]{:S(2)}) async-start(s8[6291456]{0:T(1024)(128)(4,1)} %bitcast.51), calls=%async_computation.4 | async-start | bytes 4194304
Sparse Core Ops, SparseCore 0:
  9.2 247.7 all-gather.1
where the time goes:
time: 339 us; the launch traced here: 338 us
  waiting for transfers between devices  204 us (60%)
  local copies, waits for them, and re-layouts  42.4 us (13%)
  matrix products  30.4 us (9%)
  starting transfers between devices  29 us (9%)
  other arithmetic  19.1 us (6%)
  between operations  13.5 us (4%)
    all_to_all x1, waiting for transfers between devices, fetch_rows(): lax.all_to_all(rows, 'seq', split_axis=0, concat_axis=0, tiled=True)  99.4 us
    all_gather x1, waiting for transfers between devices, body(): piece = lax.all_gather(kv_weight, 'seq', axis=2, tiled=True)  98.4 us
    unnamed x12, local copies, waits for them, and re-layouts  17.4 us
    sub x1, other arithmetic, body(): probs = jax.nn.softmax(scores, axis=-1).astype(jnp.bfloat16)  16.3 us
    all_to_all x1, starting transfers between devices, fetch_rows(): lax.all_to_all(rows, 'seq', split_axis=0, concat_axis=0, tiled=True)  13.3 us
    all_to_all x1, starting transfers between devices, fetch_rows(): lax.all_to_all(request, 'seq', split_axis=0, concat_axis=0, tiled=True)  12.7 us
    dot_general x1, matrix products, body(): jnp.einsum('cthd,cuhd->chtu', query_block, keys, preferred_element_type=j...  10.8 us
    reshape x1, local copies, waits for them, and re-layouts, body(): mixed.astype(jnp.bfloat16)  10.3 us
  transfers between devices with their start and end apart: 4, of which 4 were waited for; matrix products, arithmetic and copies ran while one was open for 5% of the time, Pallas kernels for 0%

commit v1 on v0

--- a/solution.py
+++ b/solution.py
@@ -37,7 +37,9 @@
     remote = from_partner(store, "sec", 0)
     fetched = fetch_rows(block_ids, remote, owners, slots_each, blocks_each)
     rows = fetched.reshape(-1, width)
-    piece = lax.all_gather(kv_weight, "seq", axis=2, tiled=True)
+    piece = jnp.concatenate(
+        lax.all_to_all(jnp.stack([kv_weight] * lax.axis_size("seq")), "seq", 0, 0), axis=2
+    )
     keys = jnp.dot(rows, piece[0], preferred_element_type=jnp.float32).astype(jnp.bfloat16)
     values = jnp.dot(rows, piece[1], preferred_element_type=jnp.float32).astype(jnp.bfloat16)
     projected = jnp.stack([keys, values])

time: 339 us -> 366 us (1.080); the launches traced: 338 us -> 361 us
  blocking collectives: 0 us -> 105 us
  waiting for transfers between devices: 204 us -> 132 us
  between operations: 13.5 us -> 0.12 us
  local copies, waits for them, and re-layouts: 42.4 us -> 52.2 us
  matrix products: 30.4 us -> 25.6 us
    all_to_all x0 -> x1, blocking collectives: none -> 105 us  [fetch_rows(): lax.all_to_all(rows, 'seq', split_axis=0, concat_axis=0, tiled=True)]
    all_gather x1 -> x0, waiting for transfers between devices: 98.4 us -> none  [body(): piece = lax.all_gather(kv_weight, 'seq', axis=2, tiled=True)]
    all_to_all x1, waiting for transfers between devices: 99.4 us -> 127 us  [body(): lax.all_to_all(jnp.stack([kv_weight] * lax.axis_size('seq')), 'seq', 0, 0)]
    unnamed x12 -> x16, local copies, waits for them, and re-layouts: 17.4 us -> 14.7 us
  transfers between devices with their start and end apart: 4 -> 3, of which waited for: 4 -> 3; matrix products, arithmetic and copies ran while one was open for 5% -> 4% of each run, Pallas kernels for 0% -> 0%
where the time goes in v1:
time: 366 us; the launch traced here: 361 us
  waiting for transfers between devices  132 us (36%)
  blocking collectives  105 us (29%)
  local copies, waits for them, and re-layouts  52.2 us (14%)
  starting transfers between devices  26.3 us (7%)
  matrix products  25.6 us (7%)
  other arithmetic  19.3 us (5%)
    all_to_all x1, waiting for transfers between devices, body(): lax.all_to_all(jnp.stack([kv_weight] * lax.axis_size('seq')), 'seq', 0, 0)  127 us
    all_to_all x1, blocking collectives, fetch_rows(): lax.all_to_all(rows, 'seq', split_axis=0, concat_axis=0, tiled=True)  105 us
    sub x1, other arithmetic, body(): probs = jax.nn.softmax(scores, axis=-1).astype(jnp.bfloat16)  16.5 us
    unnamed x16, local copies, waits for them, and re-layouts  14.7 us
    all_to_all x1, starting transfers between devices, fetch_rows(): lax.all_to_all(request, 'seq', split_axis=0, concat_axis=0, tiled=True)  12.7 us
    convert_element_type x1, local copies, waits for them, and re-layouts, body(): mixed.astype(jnp.bfloat16)  10.7 us
    all_to_all x1, starting transfers between devices, body(): lax.all_to_all(jnp.stack([kv_weight] * lax.axis_size('seq')), 'seq', 0, 0)  10.7 us
    dot_general x1, matrix products, body(): jnp.einsum('cthd,cuhd->chtu', query_block, keys, preferred_element_type=j...  10.7 us
  transfers between devices with their start and end apart: 3, of which 3 were waited for; matrix products, arithmetic and copies ran while one was open for 4% of the time, Pallas kernels for 0%

profile of v1, /device:TPU:98, one launch (start us, length us, event | category | flops | bytes accessed | tf_op | source)
XLA Modules:
  0.0 360.7 jit_solution(28846517541452593)
XLA Ops:
  0.0 0.8 copy.28
  0.8 0.1 reshape_squeeze.8
  0.9 0.1 fusion.15
  0.9 0.1 reduce_window_sum.11
  1.0 0.2 select_reduce_fusion.1
  1.2 0.1 select_reduce_fusion
  1.3 0.8 copy.29
  2.0 12.7 %all-to-all-start = ((s32[128,1,1]{2,1,0:T(1,128)}), s32[128,1,1]{2,1,0:T(1,128)S(1)}, u32[]{:S(2)}, u32[]{:S(2)}) async-start(s32[128,1,1]{2,1,0:T(1,128)} %copy.29), calls=%async_computation | async-start | bytes 131072 | tf_op jit(solution)/shard_map/all_to_all | solution.py:21
  14.7 3.0 collective-permute-start
  17.7 4.2 %all-to-all-done = s32[128,1,1]{2,1,0:T(1,128)S(1)} async-done(((s32[128,1,1]{2,1,0:T(1,128)}), s32[128,1,1]{2,1,0:T(1,128)S(1)}, u32[]{:S(2)}, u32[]{:S(2)}) %all-to-all-start) | async-done | bytes 544 | tf_op jit(solution)/shard_map/all_to_all | solution.py:21
  21.9 2.3 reduce
  24.3 1.1 collective-permute-done
  25.4 2.8 gather_fusion
  28.2 0.0 copy-start.3
  28.2 105.2 %all_to_all.22 = bf16[128,1,32,512]{3,2,1,0:T(8,128)(2,1)} all-to-all(bf16[128,1,32,512]{3,2,1,0:T(8,128)(2,1)} %bitcast.57), channel_id=1, replica_groups=mesh['seq'=128,'sec'=2] {'seq'}, dimensions={0} | all-to-all | bytes 8388608 | tf_op jit(solution)/shard_map/all_to_all | solution.py:23
  133.4 0.0 copy-done.3
  133.4 3.4 stack.2
  136.9 10.7 %all-to-all-start.2 = ((bf16[128,2,512,24]{2,3,1,0:T(8,128)(2,1)}), bf16[128,2,512,24]{2,3,1,0:T(8,128)(2,1)}, u32[]{:S(2)}, u32[]{:S(2)}) async-start(bf16[128,2,512,24]{2,3,1,0:T(8,128)(2,1)} %stack.2), calls=%async_computation.2 | async-start | bytes 12582912 | tf_op jit(solution)/shard_map/all_to_all | solution.py:41
  147.6 0.1 reshape_squeeze.9
  147.6 7.4 %copy.40 = bf16[128,8,24,128]{3,2,1,0:T(8,128)(2,1)} copy(bf16[128,8,24,128]{3,1,2,0:T(8,128)(2,1)} %bitcast.59) | data formatting | bytes 12582912
  155.1 3.8 %gather_fusion.1 = bf16[32,32,512]{2,1,0:T(8,128)(2,1)} fusion(bf16[128,32,512]{2,1,0:T(8,128)(2,1)} %bitcast.58, s32[1024]{0:T(1024)S(1)} %pad_clamp_fusion), kind=kCustom, calls=%fused_computation.1 | custom fusion | bytes 2097280 | tf_op jit(solution)/shard_map/gather | solution.py:25
  158.9 126.5 %all-to-all-done.2 = bf16[128,2,512,24]{2,3,1,0:T(8,128)(2,1)} async-done(((bf16[128,2,512,24]{2,3,1,0:T(8,128)(2,1)}), bf16[128,2,512,24]{2,3,1,0:T(8,128)(2,1)}, u32[]{:S(2)}, u32[]{:S(2)}) %all-to-all-start.2) | async-done | bytes 6291488 | tf_op jit(solution)/shard_map/all_to_all | solution.py:41
  285.4 3.3 copy.50
  288.7 0.0 copy-start.1
  288.7 0.0 slice-start
  288.7 2.2 fusion.19
  291.0 0.0 copy-done.1
  291.0 0.0 slice-start.1
  291.0 3.7 %convert_bitcast_fusion.1 = bf16[128,8,24,128]{3,1,2,0:T(8,128)(2,1)S(1)} fusion(bf16[1024,512]{1,0:T(8,128)(2,1)S(1)} %bitcast.63, bf16[512,3072]{0,1:T(8,128)(2,1)S(1)} %bitcast.62), kind=kOutput, calls=%fused_computation.18 | convolution fusion | flops 3224371200 | bytes 10485760 | tf_op jit(solution)/shard_map/dot_general | solution.py:43
  294.6 4.6 %copy.39 = bf16[128,8,24,128]{3,2,1,0:T(8,128)(2,1)} copy(bf16[128,8,24,128]{3,1,2,0:T(8,128)(2,1)S(1)} %convert_bitcast_fusion.1) | data formatting | bytes 12582912
  299.3 0.0 slice-done
  299.3 0.0 slice-done.1
  299.3 10.7 %fusion.8 = f32[16,24,64,64]{3,2,1,0:T(8,128)} fusion(bf16[16,64,24,128]{3,2,1,0:T(8,128)(2,1)S(1)} %bitcast.55, bf16[16,64,24,128]{3,2,1,0:T(8,128)(2,1)} %bitcast.56), kind=kOutput, calls=%fused_computation.11 | convolution fusion | flops 402653184 | bytes 18874368 | tf_op jit(solution)/shard_map/cthd,cuhd->chtu/dot_general | solution.py:51
  309.9 0.0 copy-start
  309.9 0.0 copy-start.2
  309.9 16.5 %fusion.20 = (f32[16,24,64]{2,1,0:T(8,128)S(1)}, f32[16,24,64,64]{2,3,1,0:T(8,128)}) fusion(f32[16,24,64,64]{3,2,1,0:T(8,128)} %fusion.8), kind=kOutput, calls=%fused_computation.44 | output fusion | flops 6291519 | bytes 12681216 | tf_op jit(solution)/shard_map/sub | solution.py:54
  326.4 0.0 copy-done
  326.4 0.0 copy-done.2
  326.4 3.7 %convert_bitcast_fusion.2 = bf16[128,8,24,128]{3,1,2,0:T(8,128)(2,1)S(1)} fusion(bf16[1024,512]{1,0:T(8,128)(2,1)S(1)} %bitcast.64, bf16[512,3072]{0,1:T(8,128)(2,1)S(1)} %bitcast.61), kind=kOutput, calls=%fused_computation.19 | convolution fusion | flops 3224371200 | bytes 10485760 | tf_op jit(solution)/shard_map/dot_general | solution.py:44
  330.1 1.9 copy.38
  332.1 7.6 %convert_bitcast_fusion = bf16[16,64,24,128]{3,1,2,0:T(8,128)(2,1)} fusion(f32[16,24,64,64]{2,3,1,0:T(8,128)} %get-tuple-element.10, f32[16,24,64]{2,1,0:T(8,128)S(1)} %get-tuple-element.9, bf16[16,64,24,128]{3,2,1,0:T(8,128)(2,1)S(1)} %bitcast.60), kind=kOutput, calls=%fused_computation.15 | convolution fusion | flops 408944640 | bytes 18972672 | tf_op jit(solution)/shard_map/chtu,cuhd->cthd/dot_general | solution.py:55
  339.7 10.7 %copy.36 = bf16[16,64,24,128]{3,2,1,0:T(8,128)(2,1)} copy(bf16[16,64,24,128]{3,1,2,0:T(8,128)(2,1)} %convert_bitcast_fusion) | data formatting | bytes 12582912 | tf_op jit(solution)/shard_map/convert_element_type | solution.py:56
  350.4 10.3 %reshape.192 = bf16[1,16,64,3072]{3,2,1,0:T(8,128)(2,1)} reshape(bf16[16,64,24,128]{3,2,1,0:T(8,128)(2,1)} %copy.36) | data formatting | bytes 12582912 | tf_op jit(solution)/shard_map/reshape | solution.py:56
  (7 shorter events, 0.1 us)
Async XLA Ops:
  2.0 19.9 %all-to-all-start = ((s32[128,1,1]{2,1,0:T(1,128)}), s32[128,1,1]{2,1,0:T(1,128)S(1)}, u32[]{:S(2)}, u32[]{:S(2)}) async-start(s32[128,1,1]{2,1,0:T(1,128)} %copy.29), calls=%async_computation | async-start | bytes 131072 | tf_op jit(solution)/shard_map/all_to_all | solution.py:21
  14.7 10.7 %collective-permute-start = (bf16[8,32,512]{2,1,0:T(8,128)(2,1)}, bf16[8,32,512]{2,1,0:T(8,128)(2,1)S(1)}, u32[]{:S(2)}, u32[]{:S(2)}) collective-permute-start(bf16[8,32,512]{2,1,0:T(8,128)(2,1)} %bitcast.66), channel_id=1, source_target_pairs={{0,1},{1,0},{2,3},{3,2},{4,5},{5,4},{6,7},{7,6},{8,9},{9,8},{10,11... | collective-permute-start | bytes 786440 | tf_op jit(solution)/shard_map/ppermute | solution.py:10
  28.2 105.2 %copy-start.3 = (bf16[2,512,24]{1,2,0:T(8,128)(2,1)S(1)}, bf16[2,512,24]{1,2,0:T(8,128)(2,1)}, u32[]{:S(2)}) copy-start(bf16[2,512,24]{1,2,0:T(8,128)(2,1)} %param.7) | copy-start | bytes 147460
  136.9 148.5 %all-to-all-start.2 = ((bf16[128,2,512,24]{2,3,1,0:T(8,128)(2,1)}), bf16[128,2,512,24]{2,3,1,0:T(8,128)(2,1)}, u32[]{:S(2)}, u32[]{:S(2)}) async-start(bf16[128,2,512,24]{2,3,1,0:T(8,128)(2,1)} %stack.2), calls=%async_computation.2 | async-start | bytes 12582912 | tf_op jit(solution)/shard_map/all_to_all | solution.py:41
  288.7 2.3 copy-start.1
  288.7 10.5 %slice-start = ((s8[6291456]{0:T(1024)(128)(4,1)}), s8[4194304]{0:T(1024)(128)(4,1)S(1)}, s32[]{:S(2)}) async-start(s8[6291456]{0:T(1024)(128)(4,1)} %bitcast.53), calls=%async_computation.3 | async-start | bytes 8388608
  291.0 8.3 %slice-start.1 = ((s8[6291456]{0:T(1024)(128)(4,1)}), s8[2097152]{0:T(1024)(128)(4,1)S(1)}, s32[]{:S(2)}) async-start(s8[6291456]{0:T(1024)(128)(4,1)} %bitcast.53), calls=%async_computation.4 | async-start | bytes 4194304
  309.9 16.5 %copy-start = (bf16[1,512,128,24]{1,3,2,0:T(8,128)(2,1)S(1)}, bf16[1,512,128,24]{1,3,2,0:T(8,128)(2,1)}, u32[]{:S(2)}) copy-start(bf16[1,512,128,24]{1,3,2,0:T(8,128)(2,1)} %get-tuple-element.5) | copy-start | bytes 9437188
  309.9 16.5 %copy-start.2 = (bf16[32,32,512]{2,1,0:T(8,128)(2,1)S(1)}, bf16[32,32,512]{2,1,0:T(8,128)(2,1)}, u32[]{:S(2)}) copy-start(bf16[32,32,512]{2,1,0:T(8,128)(2,1)} %gather_fusion.1) | copy-start | bytes 3145732
